TPU v7x, 256 devices: a whole 4x4x8 slice. The times are simulated.
256 devices in a mesh: col: 32 (over z, x), bin: 8 (over y, core).
Axes of the slice: x: 4, y: 4, z: 8, core: 2. Of those that a mesh axis runs over, the one named last changes fastest.
Arguments:
- slope: float32 [262144], P('bin'), may hold values from -6 to 6
- curvature: float32 [262144], P('bin'), may hold values from -6 to 0
- target_mean: float32 [262144], P('bin'), may hold values from 0.15 to 0.85
- target_var: float32 [262144], P('bin'), may hold values from 0.06 to 0.12
- table: float32 [64, 512], P(None, 'col'), may hold values from -6 to 6
Outputs:
- species_mean: float32 [64, 262144], P('col')
- final_slope: float32 [262144], replicated
All inputs are finite; a program needn't handle non-finite values.
Results may differ from a plain program's by a relative error of at most 0.0001.
Values sent between devices are 32-bit elements; how exact they have to be, the bound alone decides.
No kernel may reach another device: no remote copies, remote signals or barrier semaphores. Data moves between devices by JAX's collectives and lax.ppermute only.
A program may use at most 64 MiB of HBM per device.

v0:
```python
import jax
import jax.numpy as jnp
from jax import lax
from jax.sharding import PartitionSpec as P

ITERS = 3


def in_order(blocks, dim):
    blocks = jnp.moveaxis(blocks, 0, dim)
    shape = blocks.shape
    return blocks.reshape(*shape[:dim], shape[dim] * shape[dim + 1], *shape[dim + 2 :])


def copy_for_each(array, axis):
    copies = jnp.broadcast_to(array, (lax.axis_size(axis), *array.shape))
    return lax.all_to_all(copies, axis, split_axis=0, concat_axis=0, tiled=True)


def gather_directly(array, axis, dim):
    return in_order(copy_for_each(array, axis), dim)


def exponent(lam, curvature, points):
    return jnp.exp(lam[None, :] * points + curvature[None, :] * points * points)


def per_device(slope, curvature, target_mean, target_var, table):
    columns = lax.axis_size("col")
    width = slope.shape[0] // columns
    offset = lax.axis_index("col") * width
    own_slope = lax.dynamic_slice_in_dim(slope, offset, width, 0)
    own_curve = lax.dynamic_slice_in_dim(curvature, offset, width, 0)
    own_mean = lax.dynamic_slice_in_dim(target_mean, offset, width, 0)
    own_var = lax.dynamic_slice_in_dim(target_var, offset, width, 0)
    full_table = gather_directly(table, "col", 1)
    total_pts = full_table.shape[1]
    points = ((lax.iota(jnp.int32, total_pts).astype(jnp.float32) + 0.5) / total_pts)[:, None]
    own_lam = own_slope
    for step in range(ITERS):
        expo = exponent(own_lam, own_curve, points)
        partition = jnp.sum(expo, axis=0)
        moment = jnp.sum(points * expo, axis=0)
        own_lam = own_lam + (own_mean - moment / partition) / own_var
    expo = exponent(own_lam, own_curve, points)
    weights = expo / jnp.sum(expo, axis=0)[None, :]
    terms = jnp.dot(
        full_table, weights, precision=lax.Precision.HIGHEST, preferred_element_type=jnp.float32
    )
    species = lax.all_to_all(terms, "col", split_axis=0, concat_axis=1, tiled=True)
    lam = gather_directly(own_lam, "col", 0)
    species_mean, final_slope = (
        lax.all_gather(species, "bin", axis=1, tiled=True),
        lax.all_gather(lam, "bin", axis=0, tiled=True),
    )
    return (species_mean, final_slope)


def solution(mesh):
    placed = (P("bin"), P("bin"), P("bin"), P("bin"), P(None, "col"))
    return jax.shard_map(
        per_device, mesh=mesh, in_specs=placed, out_specs=(P("col", None), P()), check_vma=False
    )
```

profile of v0, /device:TPU:1, one launch (start us, length us, event | category | flops | bytes accessed | tf_op | source)
XLA Modules:
  0.0 104.1 jit_solution(18431287290563344208)
XLA Ops:
  7.2 0.0 copy-start
  7.2 0.0 all-gather.5.cloned.1.call-start
  7.2 0.7 dynamic_slice.14
  7.9 0.7 dynamic_slice.12
  8.6 0.7 fusion.4
  9.3 0.7 divide_add_fusion.2
  10.1 0.7 fusion
  10.8 0.7 divide_add_fusion.1
  11.5 0.7 fusion.1
  12.2 0.7 divide_add_fusion
  12.9 0.1 broadcast_in_dim.5
  13.0 21.1 %all_to_all.30 = f32[32,1,1024]{2,1,0:T(1,128)} all-to-all(f32[32,1,1024]{2,1,0:T(1,128)S(1)} %broadcast_in_dim.5), channel_id=1, replica_groups=mesh['col'=32,'bin'=8] {'col'}, dimensions={0} | all-to-all | bytes 262144 | tf_op jit(solution)/shard_map/all_to_all | solution.py:17
  34.1 0.0 all-gather.5.cloned.1.call-update
  34.1 0.0 copy-done
  34.2 0.8 reshape.32
  35.0 3.9 %all-to-all-start = ((f32[32,1,1024]{2,1,0:T(1,128)}), f32[32,1,1024]{2,1,0:T(1,128)S(1)}, u32[]{:S(2)}, u32[]{:S(2)}) async-start(f32[32,1,1024]{2,1,0:T(1,128)} %reshape.32), calls=%async_computation | async-start | bytes 262144 | tf_op jit(solution)/shard_map/all_to_all | solution.py:17
  38.9 0.0 all-gather.3.cloned.1.call-start
  38.9 0.6 fusion.3
  39.5 8.8 %all-to-all-done = f32[32,1,1024]{2,1,0:T(1,128)S(1)} async-done(((f32[32,1,1024]{2,1,0:T(1,128)}), f32[32,1,1024]{2,1,0:T(1,128)S(1)}, u32[]{:S(2)}, u32[]{:S(2)}) %all-to-all-start) | async-done | bytes 131104 | tf_op jit(solution)/shard_map/all_to_all | solution.py:17
  48.3 0.5 broadcast.18
  48.8 1.0 reduce
  49.8 0.1 reshape.33
  49.9 2.0 %fusion.7 = f32[64,1024]{1,0:T(8,128)S(1)} fusion(f32[64,512]{0,1:T(8,128)S(1)} %bitcast.15, f32[1024]{0:T(1024)S(1)} %fusion.3, f32[1024]{0:T(1024)S(1)} %divide_add_fusion, f32[1024]{0:T(1024)S(1)} %dynamic_slice.14, f32[512]{0:T(512)S(1)} %add_multiply_fusion), kind=kOutput, calls=%fused_computation.14 | convolution fusion | flops 405274624 | bytes 407552 | tf_op jit(solution)/shard_map/dot_general | solution.py:47
  51.9 0.1 all_to_all.22
  52.0 14.2 %all_to_all.31 = f32[32,2,1024]{2,1,0:T(2,128)} all-to-all(f32[32,2,1024]{2,1,0:T(2,128)S(1)} %all_to_all.22), channel_id=1, replica_groups=mesh['col'=32,'bin'=8] {'col'}, dimensions={0} | all-to-all | bytes 524288 | tf_op jit(solution)/shard_map/all_to_all | solution.py:50
  66.3 0.0 all-gather.3.cloned.1.call-update
  66.3 0.0 all-gather.5.cloned.1.call-done
  66.3 0.0 copy-start.1
  66.3 27.3 %all-gather.3.cloned.1.call-done = f32[2,262144]{1,0:T(2,128)} async-done(((f32[2,32768]{1,0:T(2,128)}), f32[2,262144]{1,0:T(2,128)}) %all-gather.3.cloned.1.call-update) | async-done | bytes 2097168 | tf_op jit(solution)/shard_map/all_gather | solution.py:53
  93.6 2.6 %copy.14 = f32[2,262144]{1,0:T(2,128)} copy(f32[2,262144]{1,0:T(2,128)} %all-gather.3.cloned.1.call-done) | data formatting | bytes 4194304
  96.2 0.0 copy-done.1
  96.2 1.0 copy.15
  (2 shorter events, 0.0 us)
Async XLA Ops:
  7.2 27.0 %copy-start = (f32[64,16]{0,1:T(8,128)S(1)}, f32[64,16]{0,1:T(8,128)}, u32[]{:S(2)}) copy-start(f32[64,16]{0,1:T(8,128)} %param.9) | copy-start | bytes 12292
  7.2 59.1 %all-gather.5.cloned.1.call-start = ((), (), s32[]{:S(2)}) async-start(), calls=%async_computation.4 | async-start | bytes 1179648 | tf_op jit(solution)/shard_map/all_gather | solution.py:54
  35.0 13.3 %all-to-all-start = ((f32[32,1,1024]{2,1,0:T(1,128)}), f32[32,1,1024]{2,1,0:T(1,128)S(1)}, u32[]{:S(2)}, u32[]{:S(2)}) async-start(f32[32,1,1024]{2,1,0:T(1,128)} %reshape.32), calls=%async_computation | async-start | bytes 262144 | tf_op jit(solution)/shard_map/all_to_all | solution.py:17
  38.9 54.7 %all-gather.3.cloned.1.call-start = ((), (), s32[]{:S(2)}) async-start(), calls=%async_computation.3 | async-start | bytes 2359296 | tf_op jit(solution)/shard_map/all_gather | solution.py:53
  66.3 29.9 %copy-start.1 = (f32[262144]{0:T(1024)S(1)}, f32[262144]{0:T(1024)}, u32[]{:S(2)}) copy-start(f32[262144]{0:T(1024)} %all-gather.5.cloned.1.call-done) | copy-start | bytes 3145732
Sparse Core Ops, SparseCore 0:
  34.3 22.9 all-gather.4
  66.4 27.1 all-gather.2
where the time goes:
time: 105 us; the launch traced here: 104 us
  waiting for transfers between devices  36.1 us (34%)
  blocking collectives  35.4 us (34%)
  between operations  14.1 us (13%)
  local copies, waits for them, and re-layouts  6.73 us (6%)
  other arithmetic  5.81 us (6%)
  starting transfers between devices  3.94 us (4%)
  matrix products  2.01 us (2%)
    all_gather x1, waiting for transfers between devices, per_device(): lax.all_gather(species, 'bin', axis=1, tiled=True)  27.3 us
    all_to_all x1, blocking collectives, copy_for_each(): return lax.all_to_all(copies, axis, split_axis=0, concat_axis=0, tiled=True)  21.1 us
    all_to_all x1, blocking collectives, per_device(): lax.all_to_all(terms, 'col', split_axis=0, concat_axis=1, tiled=True)  14.2 us
    all_to_all x1, waiting for transfers between devices, copy_for_each(): return lax.all_to_all(copies, axis, split_axis=0, concat_axis=0, tiled=True)  8.78 us
    unnamed x9, local copies, waits for them, and re-layouts  4.62 us
    all_to_all x1, starting transfers between devices, copy_for_each(): return lax.all_to_all(copies, axis, split_axis=0, concat_axis=0, tiled=True)  3.86 us
    add x3, other arithmetic, per_device(): own_lam = own_lam + (own_mean - moment / partition) / own_var  2.17 us
    reduce_sum x3, other arithmetic, per_device(): partition = jnp.sum(expo, axis=0)  2.11 us
  transfers between devices with their start and end apart: 3, of which 2 were waited for; matrix products, arithmetic and copies ran while one was open for 5% of the time, Pallas kernels for 0%

commit v1 on v0

--- a/solution.py
+++ b/solution.py
@@ -4,6 +4,12 @@
 from jax.sharding import PartitionSpec as P
 
 ITERS = 3
+
+
+def _match_flows(vector):
+    upper = jnp.stack([vector for _ in range(lax.axis_size("bin"))])
+    w_next = lax.all_to_all(upper, axis_name="bin", split_axis=0, concat_axis=0)
+    return jnp.concatenate(w_next, axis=1)
 
 
 def in_order(blocks, dim):
@@ -50,7 +56,7 @@
     species = lax.all_to_all(terms, "col", split_axis=0, concat_axis=1, tiled=True)
     lam = gather_directly(own_lam, "col", 0)
     species_mean, final_slope = (
-        lax.all_gather(species, "bin", axis=1, tiled=True),
+        _match_flows(species),
         lax.all_gather(lam, "bin", axis=0, tiled=True),
     )
     return (species_mean, final_slope)

time: 105 us -> 111 us (1.057)
  blocking collectives: 35.4 us -> 0 us
  starting transfers between devices: 3.94 us -> 30.6 us
  waiting for transfers between devices: 36.1 us -> 47.7 us
  local copies, waits for them, and re-layouts: 6.73 us -> 9.98 us
    all_to_all x2 -> x0, blocking collectives: 35.4 us -> none  [the longest x1 21.1 us: copy_for_each(): return lax.all_to_all(copies, axis, split_axis=0, concat_axis=0, tiled=True)]
    all_gather x1 -> x0, waiting for transfers between devices: 27.3 us -> none  [per_device(): lax.all_gather(species, 'bin', axis=1, tiled=True)]
    all_to_all x0 -> x2, waiting for transfers between devices: none -> 24.7 us  [the longest x1 15 us: _match_flows(): w_next = lax.all_to_all(upper, axis_name='bin', split_axis=0, concat_axis=0)]
    all_gather x1, waiting for transfers between devices: 0.02 us -> 14.3 us  [per_device(): lax.all_gather(lam, 'bin', axis=0, tiled=True)]
    all_to_all x1 -> x2, starting transfers between devices: 3.86 us -> 18 us  [copy_for_each(): return lax.all_to_all(copies, axis, split_axis=0, concat_axis=0, tiled=True)]
    all_to_all x0 -> x2, starting transfers between devices: none -> 12.5 us  [the longest x1 8.22 us: _match_flows(): w_next = lax.all_to_all(upper, axis_name='bin', split_axis=0, concat_axis=0)]
    another operation x0 -> x1, local copies, waits for them, and re-layouts: none -> 1.86 us  [_match_flows(): upper = jnp.stack([vector for _ in range(lax.axis_size('bin'))])]
    all_to_all x1 -> x2, waiting for transfers between devices: 8.78 us -> 7.98 us  [copy_for_each(): return lax.all_to_all(copies, axis, split_axis=0, concat_axis=0, tiled=True)]
  transfers between devices with their start and end apart: 3 -> 5, of which waited for: 2 -> 5; matrix products, arithmetic and copies ran while one was open for 5% -> 11% of each run, Pallas kernels for 0% -> 0%
where the time goes in v1:
time: 111 us; the launch traced here: 110 us
  waiting for transfers between devices  47.7 us (43%)
  starting transfers between devices  30.6 us (28%)
  between operations  14.1 us (13%)
  local copies, waits for them, and re-layouts  9.98 us (9%)
  other arithmetic  5.82 us (5%)
  matrix products  2.01 us (2%)
    all_to_all x2, starting transfers between devices, copy_for_each(): return lax.all_to_all(copies, axis, split_axis=0, concat_axis=0, tiled=True)  18 us
    all_to_all x1, waiting for transfers between devices, _match_flows(): w_next = lax.all_to_all(upper, axis_name='bin', split_axis=0, concat_axis=0)  15 us
    all_gather x1, waiting for transfers between devices, per_device(): lax.all_gather(lam, 'bin', axis=0, tiled=True)  14.3 us
    all_to_all x1, waiting for transfers between devices, per_device(): lax.all_to_all(terms, 'col', split_axis=0, concat_axis=1, tiled=True)  9.67 us
    all_to_all x1, starting transfers between devices, _match_flows(): w_next = lax.all_to_all(upper, axis_name='bin', split_axis=0, concat_axis=0)  8.22 us
    all_to_all x2, waiting for transfers between devices, copy_for_each(): return lax.all_to_all(copies, axis, split_axis=0, concat_axis=0, tiled=True)  7.98 us
    unnamed x11, local copies, waits for them, and re-layouts  4.65 us
    all_to_all x1, starting transfers between devices, per_device(): lax.all_to_all(terms, 'col', split_axis=0, concat_axis=1, tiled=True)  4.3 us
  transfers between devices with their start and end apart: 5, of which 5 were waited for; matrix products, arithmetic and copies ran while one was open for 11% of the time, Pallas kernels for 0%

profile of v1, /device:TPU:1, one launch (start us, length us, event | category | flops | bytes accessed | tf_op | source)
XLA Modules:
  0.0 110.2 jit_solution(5544628281906039682)
XLA Ops:
  7.2 0.0 copy-start
  7.2 0.7 copy-done
  7.9 0.8 reshape.43
  8.7 11.9 %all-to-all-start = ((f32[32,1,1024]{2,1,0:T(1,128)}), f32[32,1,1024]{2,1,0:T(1,128)S(1)}, u32[]{:S(2)}, u32[]{:S(2)}) async-start(f32[32,1,1024]{2,1,0:T(1,128)} %reshape.43), calls=%async_computation | async-start | bytes 262144 | tf_op jit(solution)/shard_map/all_to_all | solution.py:23
  20.6 0.7 dynamic_slice.14
  21.3 0.7 dynamic_slice.12
  22.0 0.7 fusion.4
  22.7 0.7 divide_add_fusion.2
  23.4 0.7 fusion
  24.2 0.7 divide_add_fusion.1
  24.9 0.7 fusion.1
  25.6 0.7 divide_add_fusion
  26.3 0.6 fusion.3
  26.9 3.1 %all-to-all-done = f32[32,1,1024]{2,1,0:T(1,128)S(1)} async-done(((f32[32,1,1024]{2,1,0:T(1,128)}), f32[32,1,1024]{2,1,0:T(1,128)S(1)}, u32[]{:S(2)}, u32[]{:S(2)}) %all-to-all-start) | async-done | bytes 131104 | tf_op jit(solution)/shard_map/all_to_all | solution.py:23
  29.9 0.7 broadcast_in_dim.5
  30.7 6.2 %all-to-all-start.3 = ((f32[32,1,1024]{2,1,0:T(1,128)}), f32[32,1,1024]{2,1,0:T(1,128)S(1)}, u32[]{:S(2)}, u32[]{:S(2)}) async-start(f32[32,1,1024]{2,1,0:T(1,128)} %broadcast_in_dim.5), calls=%async_computation.3 | async-start | bytes 262144 | tf_op jit(solution)/shard_map/all_to_all | solution.py:23
  36.8 0.5 broadcast.19
  37.4 1.0 reduce
  38.3 0.1 reshape.44
  38.4 2.0 %fusion.7 = f32[64,1024]{1,0:T(8,128)S(1)} fusion(f32[64,512]{0,1:T(8,128)S(1)} %bitcast.19, f32[1024]{0:T(1024)S(1)} %fusion.3, f32[1024]{0:T(1024)S(1)} %divide_add_fusion, f32[1024]{0:T(1024)S(1)} %dynamic_slice.14, f32[512]{0:T(512)S(1)} %add_multiply_fusion), kind=kOutput, calls=%fused_computation.14 | convolution fusion | flops 405274624 | bytes 407552 | tf_op jit(solution)/shard_map/dot_general | solution.py:53
  40.4 0.9 all_to_all.23
  41.3 4.9 %all-to-all-done.3 = f32[32,1,1024]{2,1,0:T(1,128)S(1)} async-done(((f32[32,1,1024]{2,1,0:T(1,128)}), f32[32,1,1024]{2,1,0:T(1,128)S(1)}, u32[]{:S(2)}, u32[]{:S(2)}) %all-to-all-start.3) | async-done | bytes 131104 | tf_op jit(solution)/shard_map/all_to_all | solution.py:23
  46.2 0.0 copy-start.2
  46.2 4.3 %all-to-all-start.1 = ((f32[32,2,1024]{2,1,0:T(2,128)}), f32[32,2,1024]{2,1,0:T(2,128)S(1)}, u32[]{:S(2)}, u32[]{:S(2)}) async-start(f32[32,2,1024]{2,1,0:T(2,128)} %all_to_all.23), calls=%async_computation.1 | async-start | bytes 524288 | tf_op jit(solution)/shard_map/all_to_all | solution.py:56
  50.5 0.0 all-gather.2.cloned.1.call-start
  50.5 0.0 copy-done.2
  50.6 0.7 all-gather.2.cloned.1.call-update
  51.2 9.7 %all-to-all-done.1 = f32[32,2,1024]{2,1,0:T(2,128)S(1)} async-done(((f32[32,2,1024]{2,1,0:T(2,128)}), f32[32,2,1024]{2,1,0:T(2,128)S(1)}, u32[]{:S(2)}, u32[]{:S(2)}) %all-to-all-start.1) | async-done | bytes 262176 | tf_op jit(solution)/shard_map/all_to_all | solution.py:56
  60.9 1.9 %stack.5 = f32[8,2,32768]{2,1,0:T(2,128)} broadcast(f32[2,32768]{1,0:T(2,128)S(1)} %bitcast.17), dimensions={1,2} | broadcast | bytes 2359296 | tf_op jit(solution)/shard_map/stack | solution.py:10
  62.8 8.2 %all-to-all-start.2 = ((f32[8,2,32768]{2,1,0:T(2,128)}), f32[8,2,32768]{2,1,0:T(2,128)S(1)}, u32[]{:S(2)}, u32[]{:S(2)}) async-start(f32[8,2,32768]{2,1,0:T(2,128)} %stack.5), calls=%async_computation.2 | async-start | bytes 4194304 | tf_op jit(solution)/shard_map/all_to_all | solution.py:11
  71.0 14.3 %all-gather.2.cloned.1.call-done = f32[262144]{0:T(1024)} async-done(((f32[32768]{0:T(1024)}), f32[262144]{0:T(1024)}) %all-gather.2.cloned.1.call-update) | async-done | bytes 1048592 | tf_op jit(solution)/shard_map/all_gather | solution.py:60
  85.3 15.0 %all-to-all-done.2 = f32[8,2,32768]{2,1,0:T(2,128)S(1)} async-done(((f32[8,2,32768]{2,1,0:T(2,128)}), f32[8,2,32768]{2,1,0:T(2,128)S(1)}, u32[]{:S(2)}, u32[]{:S(2)}) %all-to-all-start.2) | async-done | bytes 2097184 | tf_op jit(solution)/shard_map/all_to_all | solution.py:11
  100.3 0.0 copy-start.1
  100.3 1.3 %copy.10 = f32[2,262144]{1,0:T(2,128)} copy(f32[2,262144]{1,0:T(2,128)S(1)} %bitcast.16) | data formatting | bytes 4194304
  101.7 0.6 copy-done.1
  102.3 1.0 copy.11
  (2 shorter events, 0.0 us)
Async XLA Ops:
  7.2 0.7 copy-start
  8.7 21.2 %all-to-all-start = ((f32[32,1,1024]{2,1,0:T(1,128)}), f32[32,1,1024]{2,1,0:T(1,128)S(1)}, u32[]{:S(2)}, u32[]{:S(2)}) async-start(f32[32,1,1024]{2,1,0:T(1,128)} %reshape.43), calls=%async_computation | async-start | bytes 262144 | tf_op jit(solution)/shard_map/all_to_all | solution.py:23
  30.7 15.5 %all-to-all-start.3 = ((f32[32,1,1024]{2,1,0:T(1,128)}), f32[32,1,1024]{2,1,0:T(1,128)S(1)}, u32[]{:S(2)}, u32[]{:S(2)}) async-start(f32[32,1,1024]{2,1,0:T(1,128)} %broadcast_in_dim.5), calls=%async_computation.3 | async-start | bytes 262144 | tf_op jit(solution)/shard_map/all_to_all | solution.py:23
  46.2 4.4 %copy-start.2 = (f32[32,1,1024]{2,1,0:T(1,128)}, f32[32,1,1024]{2,1,0:T(1,128)S(1)}, u32[]{:S(2)}) copy-start(f32[32,1,1024]{2,1,0:T(1,128)S(1)} %all-to-all-done.3) | copy-start | bytes 393220
  46.2 14.7 %all-to-all-start.1 = ((f32[32,2,1024]{2,1,0:T(2,128)}), f32[32,2,1024]{2,1,0:T(2,128)S(1)}, u32[]{:S(2)}, u32[]{:S(2)}) async-start(f32[32,2,1024]{2,1,0:T(2,128)} %all_to_all.23), calls=%async_computation.1 | async-start | bytes 524288 | tf_op jit(solution)/shard_map/all_to_all | solution.py:56
  50.5 34.8 %all-gather.2.cloned.1.call-start = ((), (), s32[]{:S(2)}) async-start(), calls=%async_computation.4 | async-start | bytes 1179648 | tf_op jit(solution)/shard_map/all_gather | solution.py:60
  62.8 37.6 %all-to-all-start.2 = ((f32[8,2,32768]{2,1,0:T(2,128)}), f32[8,2,32768]{2,1,0:T(2,128)S(1)}, u32[]{:S(2)}, u32[]{:S(2)}) async-start(f32[8,2,32768]{2,1,0:T(2,128)} %stack.5), calls=%async_computation.2 | async-start | bytes 4194304 | tf_op jit(solution)/shard_map/all_to_all | solution.py:11
  100.3 2.0 %copy-start.1 = (f32[262144]{0:T(1024)S(1)}, f32[262144]{0:T(1024)}, u32[]{:S(2)}) copy-start(f32[262144]{0:T(1024)} %all-gather.2.cloned.1.call-done) | copy-start | bytes 3145732
Sparse Core Ops, SparseCore 0:
  53.2 32.0 all-gather.1
